TPU v7x, 256 devices: a whole 4x4x8 slice. The times are simulated.
256 devices in a mesh: dp: 128 (over y, z, x), rep: 2 (over core).
Axes of the slice: x: 4, y: 4, z: 8, core: 2. Of those that a mesh axis runs over, the one named last changes fastest.
Arguments:
- embeddings: float32 [131072, 1024], P(('dp', 'rep')), may hold values from -6 to 6
- cluster_ids: int32 [131072, 1], P(('dp', 'rep')), may hold values from 0 to 255; in each aligned block of 512 rows (0 to 511, 512 to 1023, ...) at most 4 rows name the same one
- boundary_slots: int32 [256, 2, 256], P(('dp', 'rep')), may hold values from 0 to 1023
Outputs:
- member_max: float32 [256, 1024], P(('dp', 'rep'))
- centrality: float32 [256, 1024], P(('dp', 'rep'))
Inputs may be any that keep to these rules, and one draw needn't show every extreme that they name: `cluster_ids`: among the rows of one device, at most 4 name the same cluster, a bound that some block reaches of them; every cluster is named by some row.
All inputs are finite; a program needn't handle non-finite values.
Results may differ from a plain program's by a relative error of at most 0.0024.
Values may be sent and summed in bfloat16 or wider, within the bound.
A program may use at most 64 MiB of HBM per device.

v0:
```python
import jax
import jax.numpy as jnp
from jax import lax
from jax.sharding import PartitionSpec as P

SLOTS = 1024
eps = 1e-06


def from_behind(array, axis, by):
    peers = lax.axis_size(axis)
    pairs = [(i, i + by) for i in range(peers) if 0 <= i + by < peers]
    return lax.ppermute(array, axis, pairs)


def per_device(embeddings, cluster_ids, boundary_slots):
    n_chips = lax.axis_size("dp")
    n_cores = lax.axis_size("rep")
    owners = n_chips * n_cores
    width = embeddings.shape[1]
    slots = SLOTS
    capacity = slots // owners
    bound = boundary_slots.shape[2]
    me = lax.axis_index(("dp", "rep"))
    labels = cluster_ids[:, 0]
    member_of = labels[:, None] == jnp.arange(owners, dtype=jnp.int32)[None, :]
    running = jnp.cumsum(member_of.astype(jnp.int32), axis=0)
    ranks = jnp.sum(jnp.where(member_of, running, 0), axis=1) - 1
    targets = labels * capacity + ranks
    unit_full = embeddings * lax.rsqrt(
        jnp.sum(embeddings * embeddings, axis=1, keepdims=True) + eps
    )
    unit_half = unit_full.astype(jnp.bfloat16)
    outgoing = jnp.zeros((slots, width), jnp.bfloat16).at[targets].set(unit_half)
    member_half = member_of.astype(jnp.bfloat16)
    shaped = outgoing.reshape(n_chips, n_cores, capacity, width)
    arrived = lax.all_to_all(
        lax.all_to_all(shaped, "dp", split_axis=0, concat_axis=0, tiled=True),
        "rep",
        split_axis=1,
        concat_axis=1,
        tiled=True,
    )
    members = arrived.reshape(slots, width)
    partial_sums = lax.dot_general(
        member_half, unit_half, (((0,), (0,)), ((), ())), preferred_element_type=jnp.float32
    )
    total = lax.psum(partial_sums, ("dp", "rep"))
    own_sum = lax.dynamic_slice_in_dim(total, me, 1, 0)
    direction = own_sum[0] * lax.rsqrt(jnp.sum(own_sum * own_sum) + eps)
    lengths = jnp.einsum("se,se->s", members, members, preferred_element_type=jnp.float32)
    filled = lengths > 0.5
    filled_int = filled.astype(jnp.int32)
    count = jnp.sum(filled_int)
    order = jnp.argsort(1 - filled_int, stable=True)
    picks = boundary_slots[0] % count
    positions = order[picks.reshape(-1)]
    outward = members[positions]
    lower = from_behind(outward[bound:], ("dp", "rep"), 1)
    upper = from_behind(outward[:bound], ("dp", "rep"), -1)
    candidates = jnp.concatenate([members, lower, upper], axis=0)
    cand_ok = jnp.concatenate(
        [filled, jnp.full((bound,), me > 0), jnp.full((bound,), me < owners - 1)]
    )
    column = jnp.arange(slots + 2 * bound, dtype=jnp.int32)
    block = min(512, slots)

    def one_block(start):
        block_rows = lax.dynamic_slice_in_dim(members, start, block, 0)
        scores = lax.dot_general(
            block_rows, candidates, (((1,), (1,)), ((), ())), preferred_element_type=jnp.float32
        )
        row_pos = start + jnp.arange(block, dtype=jnp.int32)
        keep = cand_ok[None, :] & (column[None, :] != row_pos[:, None])
        return jnp.max(jnp.where(keep, scores, -1.0), axis=1)

    starts = jnp.arange(slots // block, dtype=jnp.int32) * block
    best = lax.map(one_block, starts).reshape(slots)
    member_max = jnp.where(filled, best, 0.0)
    central = jnp.dot(
        members, direction, precision=lax.Precision.HIGHEST, preferred_element_type=jnp.float32
    )
    centrality = jnp.where(filled, central, 0.0)
    return (member_max[None, :], centrality[None, :])


def solution(mesh):
    placed = (P(("dp", "rep"), None), P(("dp", "rep"), None), P(("dp", "rep"), None, None))
    return jax.shard_map(
        per_device,
        mesh=mesh,
        in_specs=placed,
        out_specs=(P(("dp", "rep"), None), P(("dp", "rep"), None)),
        check_vma=False,
    )
```

profile of v0, /device:TPU:8, one launch (start us, length us, event | category | flops | bytes accessed | tf_op | source)
XLA Modules:
  0.0 374.8 jit_solution(14825172263603566123)
XLA Ops:
  7.2 1.8 multiply_reduce_fusion
  9.8 0.8 copy-done
  10.6 4.2 %scatter_custom_fusion = bf16[1024,1024]{1,0:T(8,128)(2,1)} fusion(s32[512]{0:T(512)S(1)} %bitcast.58, bf16[]{:T(256)} %constant.27.clone.1, f32[512,1024]{1,0:T(8,128)S(1)} %copy-done, f32[512]{0:T(512)S(1)} %add_rsqrt_fusion), kind=kCustom, calls=%fused_computation.16 | custom fusion | flops 1048576 | bytes 4196354 | tf_op jit(solution)/shard_map/scatter | solution.py:34
  14.7 4.1 %reshape.106 = bf16[128,2,4,1024]{3,2,1,0:T(4,128)(2,1)} reshape(bf16[1024,1024]{1,0:T(8,128)(2,1)} %scatter_custom_fusion) | data formatting | bytes 4194304 | tf_op jit(solution)/shard_map/reshape | solution.py:36
  18.8 15.9 %all-to-all-start = ((bf16[128,2,4,1024]{3,2,1,0:T(4,128)(2,1)}), bf16[128,2,4,1024]{3,2,1,0:T(4,128)(2,1)}, u32[]{:S(2)}, u32[]{:S(2)}) async-start(bf16[128,2,4,1024]{3,2,1,0:T(4,128)(2,1)} %reshape.106), calls=%async_computation | async-start | bytes 4194304 | tf_op jit(solution)/shard_map/all_to_all | solution.py:38
  34.8 1.7 fusion.12
  36.5 268.0 %all-reduce.2.cloned.1.call-done = f32[256,1024]{1,0:T(8,128)} async-done(((f32[256,1024]{1,0:T(8,128)}), f32[256,1024]{1,0:T(8,128)}) %all-reduce.2.cloned.1.call-update) | async-done | bytes 1048592 | tf_op jit(solution)/shard_map/psum | solution.py:48
  304.5 1.4 multiply_reduce_fusion.1
  306.6 2.3 copy.14
  308.9 5.4 %all_to_all.10 = bf16[128,2,4,1024]{3,2,0,1:T(4,128)(2,1)S(1)} all-to-all(bf16[128,2,4,1024]{3,2,0,1:T(4,128)(2,1)S(1)} %copy.14), channel_id=1, replica_groups=mesh['dp'=128,'rep'=2] {'rep'}, dimensions={1} | all-to-all | bytes 4194304 | tf_op jit(solution)/shard_map/all_to_all | solution.py:37
  314.3 2.6 copy.15
  317.0 2.5 reshape.107
  320.0 2.5 fusion.15
  322.5 0.6 broadcast_select_fusion
  323.1 0.6 convert_reduce_fusion
  325.2 4.4 %sort.17 = (s32[1024]{0:T(1024)}, s32[1024]{0:T(1024)S(1)}) sort(s32[1024]{0:T(1024)S(1)} %get-tuple-element.73, s32[1024]{0:T(1024)S(1)} %iota.25), dimensions={0}, to_apply=%region_5.6 | sort | flops 10240 | bytes 16384 | tf_op jit(solution)/shard_map/jit(argsort)/sort | solution.py:55
  329.6 2.3 gather_fusion
  331.9 2.1 gather_fusion.1
  334.0 1.1 fusion.21
  335.0 2.0 collective-permute-start
  337.1 7.7 %collective-permute-start.1 = (bf16[256,1024]{1,0:T(8,128)(2,1)}, bf16[256,1024]{1,0:T(8,128)(2,1)S(1)}, u32[]{:S(2)}, u32[]{:S(2)}) collective-permute-start(bf16[256,1024]{1,0:T(8,128)(2,1)} %get-tuple-element.71), channel_id=1, source_target_pairs={{1,0},{2,1},{3,2},{4,3},{5,4},{6,5},{7,6},{8,7},{9,8},{10,9},{11,1... | collective-permute-start | bytes 1572872 | tf_op jit(solution)/shard_map/ppermute | solution.py:13
  344.9 5.1 %collective-permute-done = bf16[256,1024]{1,0:T(8,128)(2,1)S(1)} collective-permute-done((bf16[256,1024]{1,0:T(8,128)(2,1)}, bf16[256,1024]{1,0:T(8,128)(2,1)S(1)}, u32[]{:S(2)}, u32[]{:S(2)}) %collective-permute-start) | collective-permute-done | bytes 524320 | tf_op jit(solution)/shard_map/ppermute | solution.py:13
  349.9 1.9 collective-permute-done.1
  351.8 1.9 pad_maximum_fusion
  353.7 13.6 %while.11 = (s32[]{:T(128)}, f32[2,512]{1,0:T(2,128)S(1)}, pred[1536]{0:T(1024)(128)(4,1)S(1)}, s32[2]{0:T(128)S(1)}, bf16[1024,1024]{1,0:T(8,128)(2,1)S(1)}, /*...) while((s32[]{:T(128)}, f32[2,512]{1,0:T(2,128)S(1)}, ...), condition=%wide.region_9.10_spmd.clone, body=%wide.region_7.9_spmd.clone.sunk | while | flops 1613758464 | bytes 4206743 | solution.py:78
  353.7 0.5 dynamic_slice.23
  355.9 0.5 iota_add_fusion.2
  356.4 4.0 %fusion.29 = f32[512]{0:T(512)S(1)} fusion(bf16[1536,1024]{1,0:T(8,128)(2,1)} %get-tuple-element.134, s32[512]{0:T(512)S(1)} %iota_add_fusion.2, pred[1536]{0:T(1024)(128)(4,1)S(1)} %get-tuple-element.131, bf16[1024,1024]{1,0:T(8,128)(2,1)S(1)} %get-tuple-element.133, s32[]{:T(128)S(6)} %select_n.90), kind=kOutput, calls=%fused_computation.7.clone.1 | convolution fusion | flops 1613757952 | bytes 4200452 | tf_op jit(solution)/shard_map/while/body/eval_jaxpr/dot_general | solution.py:70
  360.5 0.6 dynamic_slice.23
  362.7 0.5 iota_add_fusion.2
  363.2 4.0 %fusion.29 = f32[512]{0:T(512)S(1)} fusion(bf16[1536,1024]{1,0:T(8,128)(2,1)} %get-tuple-element.134, s32[512]{0:T(512)S(1)} %iota_add_fusion.2, pred[1536]{0:T(1024)(128)(4,1)S(1)} %get-tuple-element.131, bf16[1024,1024]{1,0:T(8,128)(2,1)S(1)} %get-tuple-element.133, s32[]{:T(128)S(6)} %select_n.90), kind=kOutput, calls=%fused_computation.7.clone.1 | convolution fusion | flops 1613757952 | bytes 4200452 | tf_op jit(solution)/shard_map/while/body/eval_jaxpr/dot_general | solution.py:70
  367.3 0.6 broadcast_select_fusion.1
  (36 shorter events, 1.6 us)
Async XLA Ops:
  7.2 1.8 copy-start.1
  9.0 1.6 copy-start
  18.8 287.7 %all-to-all-start = ((bf16[128,2,4,1024]{3,2,1,0:T(4,128)(2,1)}), bf16[128,2,4,1024]{3,2,1,0:T(4,128)(2,1)}, u32[]{:S(2)}, u32[]{:S(2)}) async-start(bf16[128,2,4,1024]{3,2,1,0:T(4,128)(2,1)} %reshape.106), calls=%async_computation | async-start | bytes 4194304 | tf_op jit(solution)/shard_map/all_to_all | solution.py:38
  34.8 269.8 %all-reduce.2.cloned.1.call-start = ((), (), s32[]{:S(2)}) async-start(), calls=%async_computation.2 | async-start | bytes 2097152 | tf_op jit(solution)/shard_map/psum | solution.py:48
  319.5 5.5 %copy-start.2 = (s32[1,2,256]{2,1,0:T(2,128)S(1)}, s32[1,2,256]{2,1,0:T(2,128)}, u32[]{:S(2)}) copy-start(s32[1,2,256]{2,1,0:T(2,128)} %param.7) | copy-start | bytes 6148
  335.0 14.9 %collective-permute-start = (bf16[256,1024]{1,0:T(8,128)(2,1)}, bf16[256,1024]{1,0:T(8,128)(2,1)S(1)}, u32[]{:S(2)}, u32[]{:S(2)}) collective-permute-start(bf16[256,1024]{1,0:T(8,128)(2,1)} %get-tuple-element.70), channel_id=1, source_target_pairs={{0,1},{1,2},{2,3},{3,4},{4,5},{5,6},{6,7},{7,8},{8,9},{9,10},{10,1... | collective-permute-start | bytes 1572872 | tf_op jit(solution)/shard_map/ppermute | solution.py:13
  337.1 14.7 %collective-permute-start.1 = (bf16[256,1024]{1,0:T(8,128)(2,1)}, bf16[256,1024]{1,0:T(8,128)(2,1)S(1)}, u32[]{:S(2)}, u32[]{:S(2)}) collective-permute-start(bf16[256,1024]{1,0:T(8,128)(2,1)} %get-tuple-element.71), channel_id=1, source_target_pairs={{1,0},{2,1},{3,2},{4,3},{5,4},{6,5},{7,6},{8,7},{9,8},{10,9},{11,1... | collective-permute-start | bytes 1572872 | tf_op jit(solution)/shard_map/ppermute | solution.py:13
Sparse Core Ops, SparseCore 0:
  41.0 263.4 all-reduce.1
where the time goes:
time: 376 us; the launch traced here: 375 us
  waiting for transfers between devices  275 us (73%)
  starting transfers between devices  25.7 us (7%)
  local copies, waits for them, and re-layouts  19.2 us (5%)
  other arithmetic  17.7 us (5%)
  between operations  16.3 us (4%)
  matrix products  12.1 us (3%)
  blocking collectives  5.42 us (1%)
    psum x1, waiting for transfers between devices, per_device(): total = lax.psum(partial_sums, ('dp', 'rep'))  268 us
    all_to_all x1, starting transfers between devices, per_device(): lax.all_to_all(shaped, 'dp', split_axis=0, concat_axis=0, tiled=True)  15.9 us
    ppermute x2, starting transfers between devices, from_behind(): return lax.ppermute(array, axis, pairs)  9.77 us
    dot_general x2, matrix products, one_block(): lax.dot_general(block_rows, candidates, (((1,), (1,)), ((), ())), preferr...  8.01 us
  transfers between devices with their start and end apart: 4, of which 3 were waited for; matrix products, arithmetic and copies ran while one was open for 1% of the time, Pallas kernels for 0%

commit v1 on v0

--- a/solution.py
+++ b/solution.py
@@ -45,7 +45,10 @@
     partial_sums = lax.dot_general(
         member_half, unit_half, (((0,), (0,)), ((), ())), preferred_element_type=jnp.float32
     )
-    total = lax.psum(partial_sums, ("dp", "rep"))
+    finish_the_patches = lambda own_rows, ax_name, peer_axis: jax.lax.psum(
+        jax.lax.psum(own_rows, ax_name), peer_axis
+    )
+    total = finish_the_patches(partial_sums, "rep", peer_axis="dp")
     own_sum = lax.dynamic_slice_in_dim(total, me, 1, 0)
     direction = own_sum[0] * lax.rsqrt(jnp.sum(own_sum * own_sum) + eps)
     lengths = jnp.einsum("se,se->s", members, members, preferred_element_type=jnp.float32)

time: 376 us -> 369 us (0.981)
  waiting for transfers between devices: 275 us -> 269 us
    psum x1 -> x2, waiting for transfers between devices: 268 us -> 262 us  [the longest x1 228 us: per_device(): jax.lax.psum(jax.lax.psum(own_rows, ax_name), peer_axis)]
  transfers between devices with their start and end apart: 4 -> 5, of which waited for: 3 -> 4; matrix products, arithmetic and copies ran while one was open for 1% -> 1% of each run, Pallas kernels for 0% -> 0%
where the time goes in v1:
time: 369 us; the launch traced here: 368 us
  waiting for transfers between devices  269 us (73%)
  starting transfers between devices  25.8 us (7%)
  local copies, waits for them, and re-layouts  19.2 us (5%)
  other arithmetic  17.7 us (5%)
  between operations  16.3 us (4%)
  matrix products  12.1 us (3%)
  blocking collectives  5.42 us (1%)
    psum x1, waiting for transfers between devices, per_device(): jax.lax.psum(jax.lax.psum(own_rows, ax_name), peer_axis)  228 us
    psum x1, waiting for transfers between devices, per_device(): jax.lax.psum(own_rows, ax_name)  33.4 us
    all_to_all x1, starting transfers between devices, per_device(): lax.all_to_all(shaped, 'dp', split_axis=0, concat_axis=0, tiled=True)  15.9 us
    ppermute x2, starting transfers between devices, from_behind(): return lax.ppermute(array, axis, pairs)  9.77 us
    dot_general x2, matrix products, one_block(): lax.dot_general(block_rows, candidates, (((1,), (1,)), ((), ())), preferr...  8.01 us
  transfers between devices with their start and end apart: 5, of which 4 were waited for; matrix products, arithmetic and copies ran while one was open for 1% of the time, Pallas kernels for 0%

profile of v1, /device:TPU:8, one launch (start us, length us, event | category | flops | bytes accessed | tf_op | source)
XLA Modules:
  0.0 368.4 jit_solution(14661034710195251544)
XLA Ops:
  7.2 1.8 multiply_reduce_fusion
  9.8 0.8 copy-done
  10.6 4.2 %scatter_custom_fusion = bf16[1024,1024]{1,0:T(8,128)(2,1)} fusion(s32[512]{0:T(512)S(1)} %bitcast.58, bf16[]{:T(256)} %constant.27.clone.1, f32[512,1024]{1,0:T(8,128)S(1)} %copy-done, f32[512]{0:T(512)S(1)} %add_rsqrt_fusion), kind=kCustom, calls=%fused_computation.16 | custom fusion | flops 1048576 | bytes 4196354 | tf_op jit(solution)/shard_map/scatter | solution.py:34
  14.7 4.1 %reshape.106 = bf16[128,2,4,1024]{3,2,1,0:T(4,128)(2,1)} reshape(bf16[1024,1024]{1,0:T(8,128)(2,1)} %scatter_custom_fusion) | data formatting | bytes 4194304 | tf_op jit(solution)/shard_map/reshape | solution.py:36
  18.8 15.9 %all-to-all-start = ((bf16[128,2,4,1024]{3,2,1,0:T(4,128)(2,1)}), bf16[128,2,4,1024]{3,2,1,0:T(4,128)(2,1)}, u32[]{:S(2)}, u32[]{:S(2)}) async-start(bf16[128,2,4,1024]{3,2,1,0:T(4,128)(2,1)} %reshape.106), calls=%async_computation | async-start | bytes 4194304 | tf_op jit(solution)/shard_map/all_to_all | solution.py:38
  34.8 1.6 fusion.12
  36.5 33.4 %all-reduce.3.cloned.1.call-done = f32[256,1024]{1,0:T(8,128)} async-done(((f32[256,1024]{1,0:T(8,128)}), f32[256,1024]{1,0:T(8,128)}) %all-reduce.3.cloned.1.call-update) | async-done | bytes 1048592 | tf_op jit(solution)/shard_map/psum | solution.py:49
  69.9 228.3 %all-reduce.5.cloned.1.call-done = f32[256,1024]{1,0:T(8,128)} async-done(((f32[256,1024]{1,0:T(8,128)}), f32[256,1024]{1,0:T(8,128)}) %all-reduce.5.cloned.1.call-update) | async-done | bytes 1048592 | tf_op jit(solution)/shard_map/psum | solution.py:48
  298.2 1.4 multiply_reduce_fusion.1
  300.3 2.3 copy.14
  302.6 5.4 %all_to_all.10 = bf16[128,2,4,1024]{3,2,0,1:T(4,128)(2,1)S(1)} all-to-all(bf16[128,2,4,1024]{3,2,0,1:T(4,128)(2,1)S(1)} %copy.14), channel_id=1, replica_groups=mesh['dp'=128,'rep'=2] {'rep'}, dimensions={1} | all-to-all | bytes 4194304 | tf_op jit(solution)/shard_map/all_to_all | solution.py:37
  308.0 2.6 copy.15
  310.7 2.5 reshape.107
  313.7 2.5 fusion.15
  316.2 0.6 broadcast_select_fusion
  316.8 0.6 convert_reduce_fusion
  318.9 4.4 %sort.17 = (s32[1024]{0:T(1024)}, s32[1024]{0:T(1024)S(1)}) sort(s32[1024]{0:T(1024)S(1)} %get-tuple-element.73, s32[1024]{0:T(1024)S(1)} %iota.25), dimensions={0}, to_apply=%region_5.6 | sort | flops 10240 | bytes 16384 | tf_op jit(solution)/shard_map/jit(argsort)/sort | solution.py:58
  323.3 2.3 gather_fusion
  325.6 2.1 gather_fusion.1
  327.7 1.1 fusion.21
  328.7 2.0 collective-permute-start
  330.8 7.7 %collective-permute-start.1 = (bf16[256,1024]{1,0:T(8,128)(2,1)}, bf16[256,1024]{1,0:T(8,128)(2,1)S(1)}, u32[]{:S(2)}, u32[]{:S(2)}) collective-permute-start(bf16[256,1024]{1,0:T(8,128)(2,1)} %get-tuple-element.71), channel_id=1, source_target_pairs={{1,0},{2,1},{3,2},{4,3},{5,4},{6,5},{7,6},{8,7},{9,8},{10,9},{11,1... | collective-permute-start | bytes 1572872 | tf_op jit(solution)/shard_map/ppermute | solution.py:13
  338.6 5.1 %collective-permute-done = bf16[256,1024]{1,0:T(8,128)(2,1)S(1)} collective-permute-done((bf16[256,1024]{1,0:T(8,128)(2,1)}, bf16[256,1024]{1,0:T(8,128)(2,1)S(1)}, u32[]{:S(2)}, u32[]{:S(2)}) %collective-permute-start) | collective-permute-done | bytes 524320 | tf_op jit(solution)/shard_map/ppermute | solution.py:13
  343.6 1.9 collective-permute-done.1
  345.5 1.9 pad_maximum_fusion
  347.4 13.6 %while.11 = (s32[]{:T(128)}, f32[2,512]{1,0:T(2,128)S(1)}, pred[1536]{0:T(1024)(128)(4,1)S(1)}, s32[2]{0:T(128)S(1)}, bf16[1024,1024]{1,0:T(8,128)(2,1)S(1)}, /*...) while((s32[]{:T(128)}, f32[2,512]{1,0:T(2,128)S(1)}, ...), condition=%wide.region_9.10_spmd.clone, body=%wide.region_7.9_spmd.clone.sunk | while | flops 1613758464 | bytes 4206743 | solution.py:81
  347.4 0.5 dynamic_slice.23
  349.6 0.5 iota_add_fusion.2
  350.1 4.0 %fusion.29 = f32[512]{0:T(512)S(1)} fusion(bf16[1536,1024]{1,0:T(8,128)(2,1)} %get-tuple-element.134, s32[512]{0:T(512)S(1)} %iota_add_fusion.2, pred[1536]{0:T(1024)(128)(4,1)S(1)} %get-tuple-element.131, bf16[1024,1024]{1,0:T(8,128)(2,1)S(1)} %get-tuple-element.133, s32[]{:T(128)S(6)} %select_n.90), kind=kOutput, calls=%fused_computation.7.clone.1 | convolution fusion | flops 1613757952 | bytes 4200452 | tf_op jit(solution)/shard_map/while/body/eval_jaxpr/dot_general | solution.py:73
  354.2 0.6 dynamic_slice.23
  356.9 4.0 %fusion.29 = f32[512]{0:T(512)S(1)} fusion(bf16[1536,1024]{1,0:T(8,128)(2,1)} %get-tuple-element.134, s32[512]{0:T(512)S(1)} %iota_add_fusion.2, pred[1536]{0:T(1024)(128)(4,1)S(1)} %get-tuple-element.131, bf16[1024,1024]{1,0:T(8,128)(2,1)S(1)} %get-tuple-element.133, s32[]{:T(128)S(6)} %select_n.90), kind=kOutput, calls=%fused_computation.7.clone.1 | convolution fusion | flops 1613757952 | bytes 4200452 | tf_op jit(solution)/shard_map/while/body/eval_jaxpr/dot_general | solution.py:73
  361.0 0.6 broadcast_select_fusion.1
  (39 shorter events, 2.2 us)
Async XLA Ops:
  7.2 1.8 copy-start.1
  9.0 1.6 copy-start
  18.8 281.4 %all-to-all-start = ((bf16[128,2,4,1024]{3,2,1,0:T(4,128)(2,1)}), bf16[128,2,4,1024]{3,2,1,0:T(4,128)(2,1)}, u32[]{:S(2)}, u32[]{:S(2)}) async-start(bf16[128,2,4,1024]{3,2,1,0:T(4,128)(2,1)} %reshape.106), calls=%async_computation | async-start | bytes 4194304 | tf_op jit(solution)/shard_map/all_to_all | solution.py:38
  34.8 35.1 %all-reduce.3.cloned.1.call-start = ((), (), s32[]{:S(2)}) async-start(), calls=%async_computation.2 | async-start | bytes 2097152 | tf_op jit(solution)/shard_map/psum | solution.py:49
  36.4 261.8 %all-reduce.5.cloned.1.call-start = ((), (), s32[]{:S(2)}) async-start(), calls=%async_computation.3 | async-start | bytes 2097152 | tf_op jit(solution)/shard_map/psum | solution.py:48
  313.2 5.5 %copy-start.2 = (s32[1,2,256]{2,1,0:T(2,128)S(1)}, s32[1,2,256]{2,1,0:T(2,128)}, u32[]{:S(2)}) copy-start(s32[1,2,256]{2,1,0:T(2,128)} %param.7) | copy-start | bytes 6148
  328.7 14.9 %collective-permute-start = (bf16[256,1024]{1,0:T(8,128)(2,1)}, bf16[256,1024]{1,0:T(8,128)(2,1)S(1)}, u32[]{:S(2)}, u32[]{:S(2)}) collective-permute-start(bf16[256,1024]{1,0:T(8,128)(2,1)} %get-tuple-element.70), channel_id=1, source_target_pairs={{0,1},{1,2},{2,3},{3,4},{4,5},{5,6},{6,7},{7,8},{8,9},{9,10},{10,1... | collective-permute-start | bytes 1572872 | tf_op jit(solution)/shard_map/ppermute | solution.py:13
  330.8 14.7 %collective-permute-start.1 = (bf16[256,1024]{1,0:T(8,128)(2,1)}, bf16[256,1024]{1,0:T(8,128)(2,1)S(1)}, u32[]{:S(2)}, u32[]{:S(2)}) collective-permute-start(bf16[256,1024]{1,0:T(8,128)(2,1)} %get-tuple-element.71), channel_id=1, source_target_pairs={{1,0},{2,1},{3,2},{4,3},{5,4},{6,5},{7,6},{8,7},{9,8},{10,9},{11,1... | collective-permute-start | bytes 1572872 | tf_op jit(solution)/shard_map/ppermute | solution.py:13
Sparse Core Ops, SparseCore 0:
  38.2 31.6 all-reduce.2
  76.1 222.1 all-reduce.4
